TPU v7x, 32 devices: a whole 2x2x4 slice. The times are simulated.
32 devices in a mesh: groups: 2 (over y), frames: 4 (over z), rows: 2 (over x), heads: 2 (over core).
Axes of the slice: x: 2, y: 2, z: 4, core: 2. Of those that a mesh axis runs over, the one named last changes fastest.
Arguments:
- queries: bfloat16 [8, 16, 64, 2240], P(('groups', 'frames'), 'rows', None, 'heads'), parts along dimension 0, may hold values from -2 to 1
- keys: bfloat16 [8, 16, 64, 2240], P(('groups', 'frames'), 'rows', None, 'heads'), parts along dimension 0, may hold values from -6 to 6
- values: bfloat16 [8, 16, 64, 2240], P(('groups', 'frames'), 'rows', None, 'heads'), parts along dimension 0, may hold values from -20 to 20
- out_weight: bfloat16 [2240, 2240], P('heads', 'frames'), may hold values from -0.125 to 0.125
Outputs:
- projected: bfloat16 [8, 16, 64, 2240], P(('groups', 'frames'), 'rows', None, 'heads'), parts along dimension 0
There are 2 independent parts, one for each index of `groups`. A program takes and returns all parts, laid end to end along the dimension named above; an argument that names none is the same for every part. Nothing has to cross between parts.
All inputs are finite; a program needn't handle non-finite values.
Results may differ from a plain program's by a relative error of at most 0.0049.
Values may be sent and summed in bfloat16 or wider, within the bound.
A program may use at most 64 MiB of HBM per device.

v0:
```python
import functools

import jax
import jax.numpy as jnp
from jax import lax
from jax.experimental import pallas as pl
from jax.experimental.pallas import tpu as pltpu
from jax.sharding import PartitionSpec as P

HD = 112
EPS = 1e-06
LANES = 128
MESH = pl.DeviceIdType.MESH


def prefix_before(local):
    position = lax.axis_index("frames") * local[0].shape[0]
    pieces = (
        lax.all_gather(local[0], "frames", axis=0, tiled=True),
        lax.all_gather(local[1], "frames", axis=0, tiled=True),
    )
    count = pieces[0].shape[0]
    keep = jnp.arange(count, dtype=jnp.int32) < position
    states = jnp.sum(jnp.where(keep[:, None, None, None], pieces[0], 0.0), axis=0, keepdims=True)
    totals = jnp.sum(jnp.where(keep[:, None, None], pieces[1], 0.0), axis=0, keepdims=True)
    return (states, totals)


def general(queries, keys, values, out_weight):
    frames_here, rows_here, columns, features = queries.shape
    heads_here = features // HD
    shape4 = (frames_here, rows_here * columns, heads_here, HD)
    query_pos = jnp.maximum(queries, 0).reshape(shape4).astype(jnp.float32)
    key_pos = jnp.maximum(keys, 0).reshape(shape4)
    value_rows = values.reshape(shape4)
    frame_state = jnp.einsum(
        "fthd,fthe->fhde", key_pos, value_rows, preferred_element_type=jnp.float32
    )
    frame_norm = jnp.sum(key_pos.astype(jnp.float32), axis=1)
    own = lax.psum((frame_state, frame_norm), "rows")
    earlier = prefix_before(own)
    state = own[0] + earlier[0]
    norm = own[1] + earlier[1]
    numer = jnp.einsum("fthd,fhde->fthe", query_pos, state, precision=lax.Precision.HIGHEST)
    denom = jnp.einsum("fthd,fhd->fth", query_pos, norm, precision=lax.Precision.HIGHEST)
    attended = (numer / (denom[..., None] + EPS)).astype(jnp.bfloat16)
    attended = attended.reshape(frames_here * rows_here * columns, features)
    terms = jnp.dot(
        attended,
        lax.all_gather(out_weight, "frames", axis=1, tiled=True),
        preferred_element_type=jnp.float32,
    )
    mixed = lax.psum_scatter(terms, "heads", scatter_dimension=1, tiled=True).astype(jnp.bfloat16)
    return mixed.reshape(frames_here, rows_here, columns, mixed.shape[1])


A, D, X, Y = 0, 1, 2, 3
PIECES = 5


def kernel(
    nz, q_hbm, k_hbm, v_hbm, w_ref, out_ref,
    q_ref, k_ref, v_ref, wbuf, att, st, own5, rs_send, rs_recv, z_recv, fin,
    in_sem, w_recv, own_send, rel_send, block_sem, rs_out, rs_in, z_out, z_in, ag_out, ag_in, at_sem,
):
    y, z = lax.axis_index("groups"), lax.axis_index("frames")
    x, c = lax.axis_index("rows"), lax.axis_index("heads")
    chunks = w_ref.shape[0]
    tokens, features = q_ref.shape
    wide = w_ref.shape[0] * w_ref.shape[1]
    heads = features // HD
    half = heads // 2
    parts = chunks // 2
    slots = nz // 2
    home = z // slots
    spot = lax.rem(z, slots)

    def dev(x_=None, y_=None, z_=None, c_=None):
        return (
            y if y_ is None else y_,
            z if z_ is None else z_,
            x if x_ is None else x_,
            c if c_ is None else c_,
        )

    x_nb, y_nb, partner = dev(x_=1 - x), dev(y_=1 - y), dev(c_=1 - c)

    loads = [
        pltpu.make_async_copy(src, dst, in_sem.at[n])
        for n, (src, dst) in enumerate(((k_hbm, k_ref), (v_hbm, v_ref), (q_hbm, q_ref)))
    ]
    for load in loads:
        load.start()

    barrier = pltpu.get_barrier_semaphore()
    greeted = [x_nb, y_nb, partner]
    for step in range(1, nz):
        for core in range(2):
            greeted.append(dev(z_=lax.rem(z + step, nz), c_=core))
    for device in greeted:
        pl.semaphore_signal(barrier, inc=1, device_id=device, device_id_type=MESH)
    pl.semaphore_wait(barrier, len(greeted))

    def remote(src, dst, send, recv, device):
        return pltpu.make_async_remote_copy(
            src_ref=src, dst_ref=dst, send_sem=send, recv_sem=recv,
            device_id=device, device_id_type=MESH,
        )

    def each(count, act, begin=0):
        def body(j, carry):
            act(j)
            return carry
        lax.fori_loop(begin, count, body, 0)

    mine = lax.rem(x + y + c, 2)
    kind = jnp.where(c == x, A, D)

    def own_copy(side, j):
        chunk = mine * parts + j
        return remote(
            w_ref.at[chunk],
            wbuf.at[spot, c, chunk],
            own_send.at[side, j],
            w_recv.at[spot, kind, j],
            dev(z_=z + 1 - 2 * side, c_=home),
        )

    def own_each(act):
        for side in range(2):
            @pl.when((z < nz - 1) if side == 0 else (z > 0))
            def _():
                each(parts, lambda j: act(own_copy(side, j)))

    @pl.when(c == x)
    def _():
        own_each(lambda copy: copy.start())

    block_local = pltpu.make_async_copy(w_ref, wbuf.at[spot, c], block_sem.at[0])
    block_out = remote(w_ref, wbuf.at[spot, c], block_sem.at[1], block_sem.at[2], partner)

    @pl.when(home == c)
    def _():
        block_local.start()

    @pl.when(home != c)
    def _():
        block_out.start()

    base = {A: (x, y * parts), D: (1 - x, (1 - y) * parts),
            X: (1 - x, y * parts), Y: (x, (1 - y) * parts)}

    def slot(i):
        s = jnp.where(z <= slots * c, i, slots - 1 - i)
        source = slots * c + s
        ends = (source == 0) | (source == nz - 1)
        return s, source, jnp.abs(source - z), ends

    def relay(s, what, j, lane, to_kind, device):
        rows, first = base[what]
        ref = wbuf.at[s, rows, first + j]
        return remote(ref, ref, rel_send.at[s, lane, j], w_recv.at[s, to_kind, j], device)

    def arrived(s, what, j):
        relay(s, what, j, 0, what, x_nb).wait_recv()

    def onward(source):
        to = jnp.where(source < z, z + 1, z - 1)
        return (to >= 0) & (to < nz), dev(z_=jnp.clip(to, 0, nz - 1))

    def relays_a(s, source, j):
        more, to = onward(source)
        return (
            (more, relay(s, A, j, 2, A, to)),
            (None, relay(s, A, j, 0, X, x_nb)),
            (None, relay(s, A, j, 1, Y, y_nb)),
        )

    def on_a(distance, j):
        for i in range(slots):
            s, source, far, ends = slot(i)

            @pl.when(far == distance)
            def _():
                arrived(s, A, j)
                for needed, copy in relays_a(s, source, j):
                    if needed is None:
                        copy.start()
                    else:
                        @pl.when(needed)
                        def _():
                            copy.start()

    def on_xy(wanted, j, only=None):
        for i in range(slots) if only is None else (only,):
            s, source, far, ends = slot(i)
            by_x = (3 * parts) // PIECES

            @pl.when((far > 0) & wanted(far, ends))
            def _():
                arrived(s, X, j)
                arrived(s, Y, j)

                @pl.when(jnp.logical_not(ends) & (j < by_x))
                def _():
                    relay(s, Y, j, 3, D, x_nb).start()

                @pl.when(jnp.logical_not(ends) & (j >= by_x))
                def _():
                    relay(s, X, j, 3, D, y_nb).start()

    def on_d(i, wanted, j):
        s, source, far, ends = slot(i)

        @pl.when((far > 0) & wanted(far, ends))
        def _():
            arrived(s, D, j)
            more, to = onward(source)

            @pl.when(ends & more)
            def _():
                relay(s, D, j, 3, D, to).start()

    def on_block(i):
        s, source, far, ends = slot(i)

        @pl.when(far == 0)
        def _():
            block_local.wait()
            other = wbuf.at[spot, 1 - c]
            remote(w_ref, other, block_sem.at[1], block_sem.at[2], partner).wait_recv()

    def drain(i):
        s, source, far, ends = slot(i)
        more, to = onward(source)

        def one(j):
            for needed, copy in relays_a(s, source, j):
                if needed is None:
                    copy.wait_send()
                else:
                    @pl.when(needed)
                    def _():
                        copy.wait_send()

            @pl.when(jnp.logical_not(ends) | more)
            def _():
                relay(s, X, j, 3, D, y_nb).wait_send()

        @pl.when(far > 0)
        def _():
            each(parts, one)

    def rs(j):
        return remote(rs_send.at[j], rs_recv.at[j], rs_out.at[j], rs_in.at[j], x_nb)

    loads[0].wait()
    loads[1].wait()
    ones = jnp.ones((tokens, LANES), jnp.bfloat16)
    for j in range(half):
        for h in (j, half + j):
            cols = slice(h * HD, (h + 1) * HD)
            kp = jnp.maximum(k_ref[:, cols], 0)
            dims = (((0,), (0,)), ((), ()))
            st[h, :, :HD] = lax.dot_general(
                kp, v_ref[:, cols], dims, preferred_element_type=jnp.float32)
            total = lax.dot_general(kp, ones, dims, preferred_element_type=jnp.float32)
            st[h, :, HD:] = total[:, HD:]
        rs_send[j] = st[(1 - x) * half + j].astype(jnp.bfloat16)
        rs(j).start()
        on_a(1, j)

    def up(j):
        return remote(fin.at[x * half + j], z_recv.at[j], z_out.at[j], z_in.at[j],
                      dev(z_=jnp.minimum(z + 1, nz - 1)))

    def across(j):
        ref = fin.at[x * half + j]
        return remote(ref, ref, ag_out.at[j], ag_in.at[j], x_nb)

    def finish(j, total):
        fin[x * half + j] = total.astype(jnp.bfloat16)

        @pl.when(z < nz - 1)
        def _():
            up(j).start()
        across(j).start()

    @pl.when((c != x) & ((z == 0) | (z == nz - 1)))
    def _():
        own_each(lambda copy: copy.start())

    def near_step(j):
        rs(j).wait_recv()
        total = st[x * half + j] + rs_recv[j].astype(jnp.float32)
        own5[j] = total

        @pl.when(z == 0)
        def _():
            finish(j, total)

    def next_step(j):
        on_a(2, j)
        on_xy(lambda far, ends: (far == 1) & jnp.logical_not(ends), j)

    def chain_step(j):
        @pl.when(z > 0)
        def _():
            up(j).wait_recv()
            finish(j, own5[j] + z_recv[j].astype(jnp.float32))

    def far_step(j):
        on_a(3, j)
        for i in range(slots):
            on_d(i, lambda far, ends: (far == 1) & ends, j)
        on_xy(lambda far, ends: (far == 2) & jnp.logical_not(ends), j)

    def last_step(j):
        for i in range(slots):
            on_d(i, lambda far, ends: (far == 2) & ends, j)

    each(half, near_step)
    each(parts, next_step)
    each(half, chain_step)
    each(parts, far_step)
    each(parts, last_step)

    def across_in(j):
        ref = fin.at[(1 - x) * half + j]
        remote(ref, ref, ag_out.at[j], ag_in.at[j], x_nb).wait_recv()

    each(half, across_in)

    loads[2].wait()
    for h in range(heads):
        qp = jnp.maximum(q_ref[:, h * HD:(h + 1) * HD], 0)
        both = jnp.dot(qp, fin[h], preferred_element_type=jnp.float32)
        share = both[:, :HD] / (both[:, HD:HD + 1] + EPS)
        att[c, :, h * HD:(h + 1) * HD] = share.astype(jnp.bfloat16)
    att_out = remote(att.at[c], att.at[c], at_sem.at[0], at_sem.at[1], partner)
    att_out.start()
    remote(att.at[1 - c], att.at[1 - c], at_sem.at[0], at_sem.at[1], partner).wait_recv()

    for i in range(slots):
        s = slot(i)[0]
        on_block(i)
        each(parts, lambda j: on_xy(lambda far, ends: ends, j, i))
        each(parts, lambda j: on_d(
            i, lambda far, ends: (far > 2) | jnp.logical_not(ends), j))
        out = None
        for r in range(2):
            part = lax.dot_general(
                att[r], wbuf[s, r].reshape(wide, features),
                (((1,), (1,)), ((), ())), preferred_element_type=jnp.float32,
            )
            out = part if out is None else out + part
        out = out.astype(out_ref.dtype)
        for place in range(slots):
            @pl.when(s == place)
            def _():
                out_ref[:, place * wide:(place + 1) * wide] = out

    @pl.when((c == x) | (z == 0) | (z == nz - 1))
    def _():
        own_each(lambda copy: copy.wait_send())

    @pl.when(home != c)
    def _():
        block_out.wait_send()

    def sent(j):
        rs(j).wait_send()
        across(j).wait_send()

        @pl.when(z < nz - 1)
        def _():
            up(j).wait_send()

    each(half, sent)
    att_out.wait_send()
    for i in range(slots):
        drain(i)


def fused(nz, queries, keys, values, out_weight):
    frames_here, rows_here, columns, features = queries.shape
    tokens = frames_here * rows_here * columns
    heads, half, wide = features // HD, features // HD // 2, out_weight.shape[1]
    slots = nz // 2
    chunks = 2 * PIECES
    parts = PIECES
    width = wide // chunks
    vmem, hbm = pl.BlockSpec(memory_space=pltpu.VMEM), pl.BlockSpec(memory_space=pl.ANY)
    bf16, f32 = jnp.bfloat16, jnp.float32
    dma = pltpu.SemaphoreType.DMA
    out = pl.pallas_call(
        functools.partial(kernel, nz),
        out_shape=jax.ShapeDtypeStruct((tokens, slots * wide), bf16),
        in_specs=[hbm] * 4,
        out_specs=vmem,
        scratch_shapes=[
            pltpu.VMEM((tokens, features), bf16),
            pltpu.VMEM((tokens, features), bf16),
            pltpu.VMEM((tokens, features), bf16),
            pltpu.VMEM((slots, 2, chunks, width, features), bf16),
            pltpu.VMEM((2, tokens, features), bf16),
            pltpu.VMEM((heads, HD, LANES), f32),
            pltpu.VMEM((half, HD, LANES), f32),
            pltpu.VMEM((half, HD, LANES), bf16),
            pltpu.VMEM((half, HD, LANES), bf16),
            pltpu.VMEM((half, HD, LANES), bf16),
            pltpu.VMEM((heads, HD, LANES), bf16),
            dma((3,)),
            dma((slots, 4, parts)),
            dma((2, parts)),
            dma((slots, 4, parts)),
            dma((3,)),
            dma((half,)),
            dma((half,)),
            dma((half,)),
            dma((half,)),
            dma((half,)),
            dma((half,)),
            dma((2,)),
        ],
        compiler_params=pltpu.CompilerParams(
            collective_id=0, has_side_effects=True, vmem_limit_bytes=56 * 2**20),
        name="attend_project",
    )(
        queries.reshape(tokens, features),
        keys.reshape(tokens, features),
        values.reshape(tokens, features),
        out_weight.T.reshape(chunks, width, features),
    )
    return out.reshape(frames_here, rows_here, columns, slots * wide)


def solution(mesh):
    size = dict(mesh.shape)
    pairs = size["rows"] == 2 and size["groups"] == 2 and size["heads"] == 2
    body = general
    if pairs and size["frames"] == 4:
        body = functools.partial(fused, size["frames"])
    return jax.shard_map(
        body,
        mesh=mesh,
        in_specs=(
            P(("groups", "frames"), "rows", None, "heads"),
            P(("groups", "frames"), "rows", None, "heads"),
            P(("groups", "frames"), "rows", None, "heads"),
            P("heads", "frames"),
        ),
        out_specs=P(("groups", "frames"), "rows", None, "heads"),
        check_vma=False,
    )
```

profile of v0, /device:TPU:24, one launch (start us, length us, event | category | flops | bytes accessed | tf_op | source)
XLA Modules:
  0.0 56.5 jit_solution(305828989890828546)
XLA Ops:
  0.0 54.1 %attend_project.1 = bf16[512,1120]{1,0:T(8,128)(2,1)} custom-call(bf16[512,1120]{1,0:T(8,128)(2,1)} %bitcast.9, bf16[512,1120]{1,0:T(8,128)(2,1)} %bitcast.10, bf16[512,1120]{1,0:T(8,128)(2,1)} %bitcast.11, bf16[10,56,1120]{2,1,0:T(8,128)(2,1)} %bitcast.8), custom_call_target="tpu_custom_call" | custom-call | tf_op jit(solution)/shard_map/attend_project/pallas_call | solution.py:396
  54.1 2.4 %copy.6 = bf16[1,8,64,1120]{3,2,1,0:T(8,128)(2,1)} copy(bf16[1,8,64,1120]{3,2,1,0:T(8,128)(2,1)} %bitcast.7) | data formatting | bytes 2293760
where the time goes:
time: 56.6 us; the launch traced here: 56.5 us
  Pallas kernels  54.1 us (96%)
  local copies, waits for them, and re-layouts  2.37 us (4%)
    pallas_call x1, Pallas kernels, fused(): pl.pallas_call(functools.partial(kernel, nz), out_shape=jax.ShapeDtypeStr...  54.1 us
    unnamed x1, local copies, waits for them, and re-layouts  2.37 us

commit v1 on v0

v1 whole, which is shorter than its diff:
```python
import functools

import jax
import jax.numpy as jnp
from jax import lax
from jax.experimental import pallas as pl
from jax.experimental.pallas import tpu as pltpu
from jax.sharding import PartitionSpec as P

HD = 112
EPS = 1e-06
LANES = 128
MESH = pl.DeviceIdType.MESH


def prefix_before(local):
    position = lax.axis_index("frames") * local[0].shape[0]
    pieces = (
        lax.all_gather(local[0], "frames", axis=0, tiled=True),
        lax.all_gather(local[1], "frames", axis=0, tiled=True),
    )
    count = pieces[0].shape[0]
    keep = jnp.arange(count, dtype=jnp.int32) < position
    states = jnp.sum(jnp.where(keep[:, None, None, None], pieces[0], 0.0), axis=0, keepdims=True)
    totals = jnp.sum(jnp.where(keep[:, None, None], pieces[1], 0.0), axis=0, keepdims=True)
    return (states, totals)


def general(queries, keys, values, out_weight):
    frames_here, rows_here, columns, features = queries.shape
    heads_here = features // HD
    shape4 = (frames_here, rows_here * columns, heads_here, HD)
    query_pos = jnp.maximum(queries, 0).reshape(shape4).astype(jnp.float32)
    key_pos = jnp.maximum(keys, 0).reshape(shape4)
    value_rows = values.reshape(shape4)
    frame_state = jnp.einsum(
        "fthd,fthe->fhde", key_pos, value_rows, preferred_element_type=jnp.float32
    )
    frame_norm = jnp.sum(key_pos.astype(jnp.float32), axis=1)
    own = lax.psum((frame_state, frame_norm), "rows")
    earlier = prefix_before(own)
    state = own[0] + earlier[0]
    norm = own[1] + earlier[1]
    numer = jnp.einsum("fthd,fhde->fthe", query_pos, state, precision=lax.Precision.HIGHEST)
    denom = jnp.einsum("fthd,fhd->fth", query_pos, norm, precision=lax.Precision.HIGHEST)
    attended = (numer / (denom[..., None] + EPS)).astype(jnp.bfloat16)
    attended = attended.reshape(frames_here * rows_here * columns, features)
    terms = jnp.dot(
        attended,
        lax.all_gather(out_weight, "frames", axis=1, tiled=True),
        preferred_element_type=jnp.float32,
    )
    mixed = lax.psum_scatter(terms, "heads", scatter_dimension=1, tiled=True).astype(jnp.bfloat16)
    return mixed.reshape(frames_here, rows_here, columns, mixed.shape[1])


A, D, X, Y = 0, 1, 2, 3
PIECES = 5
OVER_Z, OVER_X, LAG = 1, 2, 3


def kernel(
    nz, q_hbm, k_hbm, v_hbm, w_ref, out_ref,
    q_ref, k_ref, v_ref, kt, wbuf, att, st, acc, rs_send, rs_recv, hand, z_recv, fin_send, fin, fmat, nmat,
    in_sem, w_recv, own_send, rel_send, block_sem, rs_out, rs_in, hand_out, hand_in, z_out, z_in,
    ag_out, give_out, fin_in, at_out, at_in,
):
    y, z = lax.axis_index("groups"), lax.axis_index("frames")
    x, c = lax.axis_index("rows"), lax.axis_index("heads")
    chunks = w_ref.shape[0]
    tokens, features = q_ref.shape
    wide = w_ref.shape[0] * w_ref.shape[1]
    heads = features // HD
    half = heads // 2
    parts = chunks // 2
    slots = nz // 2
    home = z // slots
    relays = c == x
    f32, bf16 = jnp.float32, jnp.bfloat16

    def dev(x_=None, y_=None, z_=None, c_=None):
        return (
            y if y_ is None else y_,
            z if z_ is None else z_,
            x if x_ is None else x_,
            c if c_ is None else c_,
        )

    partner = dev(c_=1 - c)
    barrier = pltpu.get_barrier_semaphore()

    def greet(device):
        pl.semaphore_signal(barrier, inc=1, device_id=device, device_id_type=MESH)

    greet(partner)
    for core in range(2):
        greet(dev(x_=1 - x, c_=core))
        greet(dev(y_=1 - y, c_=core))
    for side in (-1, 1):
        @pl.when((z + side >= 0) & (z + side < nz))
        def _():
            for core in range(2):
                greet(dev(z_=z + side, c_=core))

    loads = [
        pltpu.make_async_copy(src, dst, in_sem.at[n])
        for n, (src, dst) in enumerate(((k_hbm, k_ref), (v_hbm, v_ref), (q_hbm, q_ref)))
    ]
    for load in loads:
        load.start()

    pl.semaphore_wait(barrier, jnp.where((z > 0) & (z < nz - 1), 9, 7))

    def remote(src, dst, send, recv, device):
        return pltpu.make_async_remote_copy(
            src_ref=src, dst_ref=dst, send_sem=send, recv_sem=recv,
            device_id=device, device_id_type=MESH,
        )

    def each(count, act, begin=0):
        def body(j, carry):
            act(j)
            return carry
        lax.fori_loop(begin, count, body, 0)

    def when(wanted, act):
        @pl.when(wanted)
        def _():
            act()

    mine = lax.rem(x + y + c, 2)
    kind = jnp.where(relays, A, D)

    def own_copy(side, j):
        chunk = mine * parts + j
        return remote(
            w_ref.at[chunk],
            wbuf.at[z, c, chunk],
            own_send.at[side, j],
            w_recv.at[z, kind, j],
            dev(z_=z + 1 - 2 * side, c_=x),
        )

    def own_each(act):
        for side in range(2):
            @pl.when((z < nz - 1) if side == 0 else (z > 0))
            def _():
                each(parts, lambda j: act(own_copy(side, j)))

    when(relays, lambda: own_each(lambda copy: copy.start()))

    def near_copy(j):
        chunk = mine * parts + j
        return remote(
            w_ref.at[chunk],
            wbuf.at[z, c, chunk],
            own_send.at[2, j],
            w_recv.at[z, D, j],
            dev(z_=jnp.where(z == 1, 0, nz - 1), c_=home),
        )

    def near_each(act):
        @pl.when(jnp.logical_not(relays) & ((z == 1) | (z == nz - 2)))
        def _():
            each(OVER_Z, lambda j: act(near_copy(j)))

    near_each(lambda copy: copy.start())

    block_local = pltpu.make_async_copy(w_ref, wbuf.at[z, c], block_sem.at[0])
    block_out = remote(w_ref, wbuf.at[z, c], block_sem.at[1], block_sem.at[2], partner)
    when(home == c, block_local.start)
    when(home != c, block_out.start)

    base = {A: (x, y * parts), D: (1 - x, (1 - y) * parts),
            X: (1 - x, y * parts), Y: (x, (1 - y) * parts)}

    def relay(s, what, j, lane, to_kind, device):
        rows, first = base[what]
        ref = wbuf.at[s, rows, first + j]
        return remote(ref, ref, rel_send.at[s, lane, j], w_recv.at[s, to_kind, j], device)

    def arrived(s, what, j):
        relay(s, what, j, 0, what, partner).wait_recv()

    def place(s):
        to = jnp.where(s < z, z + 1, z - 1)
        then = jnp.where(s < z, z + 2, z - 2)
        ends = (s == 0) | (s == nz - 1)
        more = (to >= 0) & (to < nz)
        last = (then < 0) | (then >= nz)
        return ends, more, last, jnp.clip(to, 0, nz - 1), s // slots

    edge = (z == 0) | (z == nz - 1)

    def split(s, j):
        direct = jnp.where(edge & (jnp.abs(s - z) == 1), OVER_Z, 0)
        plane = (s > 0) & (s < nz - 1) & (j >= direct)
        return plane & (j < direct + OVER_X), plane & (j >= direct + OVER_X)

    def sends_a(s, j):
        ends, more, last, to, at = place(s)
        over_x, over_y = split(s, j)
        x_core = jnp.where(over_y, 1 - x, at)
        y_core = jnp.where(over_x, x, at)
        return (
            (more, relay(s, A, j, 2, A, dev(z_=to, c_=x))),
            (None, relay(s, A, j, 0, X, dev(x_=1 - x, c_=x_core))),
            (None, relay(s, A, j, 1, Y, dev(y_=1 - y, c_=y_core))),
            (at != x, relay(s, A, j, 4, A, partner)),
        )

    def sends_d(s, j):
        ends, more, last, to, at = place(s)
        far = ends & more
        over_x, over_y = split(s, j)
        z_core = jnp.where(last, at, x)
        return (
            (over_x, Y, relay(s, Y, j, 3, D, dev(x_=1 - x, c_=at)), relay(s, Y, j, 5, Y, partner)),
            (over_y, X, relay(s, X, j, 3, D, dev(y_=1 - y, c_=at)), relay(s, X, j, 5, X, partner)),
            (far, D, relay(s, D, j, 3, D, dev(z_=to, c_=z_core)), relay(s, D, j, 5, D, partner)),
        ), at != x

    def around(d, act):
        for side in (-1, 1):
            s = z + side * d
            when((s >= 0) & (s < nz), lambda: act(jnp.clip(s, 0, nz - 1)))

    def on_a(s, j):
        arrived(s, A, j)
        for needed, copy in sends_a(s, j):
            if needed is None:
                copy.start()
            else:
                when(needed, copy.start)

    def on_d(s, j):
        options, share = sends_d(s, j)
        for wanted, what, copy, inner in options:
            @pl.when(wanted)
            def _():
                arrived(s, what, j)
                copy.start()
                when(share, inner.start)

    def drain(s, j):
        for needed, copy in sends_a(s, j):
            if needed is None:
                copy.wait_send()
            else:
                when(needed, copy.wait_send)
        options, share = sends_d(s, j)
        for wanted, what, copy, inner in options:
            @pl.when(wanted)
            def _():
                copy.wait_send()
                when(share, inner.wait_send)

    def rs(j):
        return remote(rs_send.at[(1 - x) * half + j], rs_recv.at[c, j], rs_out.at[j], rs_in.at[c, j],
                      dev(x_=1 - x, c_=x))

    def give(j):
        return remote(rs_send.at[x * half + j], hand.at[j], hand_out.at[j], hand_in.at[j], partner)

    loads[0].wait()
    kt[...] = jnp.maximum(k_ref[...], 0).T
    loads[1].wait()
    ones = jnp.ones((tokens, LANES), bf16)
    for j in range(half):
        for h in (j, half + j):
            first = h * HD
            begin = first // LANES * LANES
            end = min(-(-(first + HD) // LANES) * LANES, features)
            kp = kt[first:first + HD, :]
            both = jnp.dot(kp, v_ref[:, begin:end], preferred_element_type=f32)
            total = jnp.dot(kp, ones, preferred_element_type=f32)
            st[h, :, :HD] = both[:, first - begin:first - begin + HD]
            st[h, :, HD:] = total[:, HD:]
            rs_send[h] = st[h].astype(bf16)
        rs(j).start()
        when(relays, give(j).start)

    fmat[...] = jnp.zeros_like(fmat)
    nmat[...] = jnp.zeros_like(nmat)

    def up(core, j):
        return remote(fin_send.at[core, j], z_recv.at[core, j], z_out.at[core, j], z_in.at[core, j],
                      dev(z_=jnp.minimum(z + 1, nz - 1)))

    def across(core, j):
        return remote(fin_send.at[core, j], fin.at[x * half + j], ag_out.at[core, j], fin_in.at[x * half + j],
                      dev(x_=1 - x, c_=core))

    def inner(core, j):
        return remote(fin_send.at[core, j], fin.at[x * half + j], give_out.at[j], fin_in.at[x * half + j],
                      partner)

    def gather_step(j):
        for core in range(2):
            pltpu_wait = remote(rs_recv.at[core, j], rs_recv.at[core, j], rs_out.at[j], rs_in.at[core, j], partner)
            pltpu_wait.wait_recv()

            @pl.when(c == core)
            def _():
                acc[core, j] = st[x * half + j] + rs_recv[core, j].astype(f32)

            @pl.when(c != core)
            def _():
                give(j).wait_recv()
                acc[core, j] = hand[j].astype(f32) + rs_recv[core, j].astype(f32)

    def chain_step(j):
        for core in range(2):
            @pl.when(z > 0)
            def _():
                up(core, j).wait_recv()
                acc[core, j] = acc[core, j] + z_recv[core, j].astype(f32)
            fin_send[core, j] = acc[core, j].astype(bf16)
            when(z < nz - 1, up(core, j).start)
            across(core, j).start()

            @pl.when(c == core)
            def _():
                fin[x * half + j] = fin_send[core, j]
            when(c != core, inner(core, j).start)

    @pl.when(jnp.logical_not(relays))
    def _():
        each(half, gather_step)
        when(z == nz - 1, lambda: own_each(lambda copy: copy.start()))
        each(half, chain_step)
        when(z == 0, lambda: own_each(lambda copy: copy.start()))

    cuts = []
    for begin in range(0, features, 2 * LANES):
        end = min(begin + 2 * LANES, features)
        low = begin // HD * HD // LANES * LANES
        high = min(-(-(-(-end // HD) * HD) // LANES) * LANES, features)
        cuts.append((begin, end, low, high))

    def finished(i):
        ref = fin.at[i]
        remote(ref, ref, give_out.at[0], fin_in.at[i], partner).wait_recv()

    sections = ((0, 4 * LANES), (4 * LANES, features))

    def att_copy(n, rows):
        begin, end = sections[n]
        ref = att.at[rows, :, begin:end]
        return remote(ref, ref, at_out.at[n], at_in.at[n], partner)

    def attend():
        each(half, lambda j: finished((1 - x) * half + j))
        when(relays, lambda: each(half, lambda j: finished(x * half + j)))
        for h in range(heads):
            own = slice(h * HD, (h + 1) * HD)
            fmat[own, own] = fin[h, :, :HD]
            nmat[own, own] = jnp.broadcast_to(fin[h, :, HD:HD + 1], (HD, HD))
        sent = 0
        for begin, end, low, high in cuts:
            qp = jnp.maximum(q_ref[:, low:high], 0)
            numer = jnp.dot(qp, fmat[low:high, begin:end], preferred_element_type=f32)
            denom = jnp.dot(qp, nmat[low:high, begin:end], preferred_element_type=f32)
            att[c, :, begin:end] = (numer / (denom + EPS)).astype(bf16)
            if end == sections[sent][1]:
                att_copy(sent, c).start()
                sent += 1

    loads[2].wait()
    turn = jnp.where(relays, parts + (parts - 2) * z, 0)

    def step(t):
        d, j = t // parts + 1, lax.rem(t, parts)

        @pl.when(relays)
        def _():
            when(d < nz, lambda: around(d, lambda s: on_a(s, j)))
            late = t - LAG

            @pl.when(late >= 0)
            def _():
                around(late // parts + 1, lambda s: on_d(s, lax.rem(late, parts)))
        when(t == turn, attend)

    each((nz - 1) * parts + LAG, step)

    for n in range(len(sections)):
        att_copy(n, 1 - c).wait_recv()

    def slot(i):
        s = jnp.where(z <= slots * c, i, slots - 1 - i)
        return s, slots * c + s

    def landed(s, j, kinds):
        ends, more, last, to, at = place(s)
        over_x, over_y = split(s, j)
        held = {A: relays, X: relays & over_y, Y: relays & over_x, D: relays & ends & more}
        for what in kinds:
            when(jnp.logical_not(held[what]), lambda: arrived(s, what, j))

    def product(rows, weights):
        return lax.dot_general(att[rows], weights, (((1,), (1,)), ((), ())), preferred_element_type=f32)

    width = wide // 2
    for i in range(slots):
        s, source = slot(i)

        def quarter(rows, first):
            return wbuf[source, rows, pl.ds(first, parts)].reshape(width, features)

        def await_all(kinds):
            @pl.when(source != z)
            def _():
                each(parts, lambda j: landed(source, j, kinds))

        @pl.when(source == z)
        def _():
            block_local.wait()
            other = wbuf.at[z, 1 - c]
            remote(w_ref, other, block_sem.at[1], block_sem.at[2], partner).wait_recv()

        def put(side, value):
            value = value.astype(out_ref.dtype)
            for at in range(slots):
                for part in range(2):
                    first = (at * 2 + part) * width

                    @pl.when((s == at) & (side == part))
                    def _():
                        out_ref[:, first:first + width] = value

        await_all((A, X))
        put(y, product(x, quarter(x, y * parts)) + product(1 - x, quarter(1 - x, y * parts)))
        await_all((Y,))
        rest = product(x, quarter(x, (1 - y) * parts))
        await_all((D,))
        put(1 - y, rest + product(1 - x, quarter(1 - x, (1 - y) * parts)))

    near_each(lambda copy: copy.wait_send())
    when(relays | (z == 0) | (z == nz - 1), lambda: own_each(lambda copy: copy.wait_send()))
    when(home != c, block_out.wait_send)

    def sent(j):
        rs(j).wait_send()
        when(relays, give(j).wait_send)

        @pl.when(jnp.logical_not(relays))
        def _():
            for core in range(2):
                when(z < nz - 1, up(core, j).wait_send)
                across(core, j).wait_send()
                when(c != core, inner(core, j).wait_send)

    each(half, sent)
    for n in range(len(sections)):
        att_copy(n, c).wait_send()

    @pl.when(relays)
    def _():
        def drained(t):
            around(t // parts + 1, lambda s: drain(s, lax.rem(t, parts)))
        each((nz - 1) * parts, drained)


def fused(nz, queries, keys, values, out_weight):
    frames_here, rows_here, columns, features = queries.shape
    tokens = frames_here * rows_here * columns
    heads, half, wide = features // HD, features // HD // 2, out_weight.shape[1]
    slots = nz // 2
    chunks = 2 * PIECES
    parts = PIECES
    width = wide // chunks
    vmem, hbm = pl.BlockSpec(memory_space=pltpu.VMEM), pl.BlockSpec(memory_space=pl.ANY)
    bf16, f32 = jnp.bfloat16, jnp.float32
    dma = pltpu.SemaphoreType.DMA
    out = pl.pallas_call(
        functools.partial(kernel, nz),
        out_shape=jax.ShapeDtypeStruct((tokens, slots * wide), bf16),
        in_specs=[hbm] * 4,
        out_specs=vmem,
        scratch_shapes=[
            pltpu.VMEM((tokens, features), bf16),
            pltpu.VMEM((tokens, features), bf16),
            pltpu.VMEM((tokens, features), bf16),
            pltpu.VMEM((features, tokens), bf16),
            pltpu.VMEM((nz, 2, chunks, width, features), bf16),
            pltpu.VMEM((2, tokens, features), bf16),
            pltpu.VMEM((heads, HD, LANES), f32),
            pltpu.VMEM((2, half, HD, LANES), f32),
            pltpu.VMEM((heads, HD, LANES), bf16),
            pltpu.VMEM((2, half, HD, LANES), bf16),
            pltpu.VMEM((half, HD, LANES), bf16),
            pltpu.VMEM((2, half, HD, LANES), bf16),
            pltpu.VMEM((2, half, HD, LANES), bf16),
            pltpu.VMEM((heads, HD, LANES), bf16),
            pltpu.VMEM((features, features), bf16),
            pltpu.VMEM((features, features), bf16),
            dma((3,)),
            dma((nz, 4, parts)),
            dma((3, parts)),
            dma((nz, 6, parts)),
            dma((3,)),
            dma((half,)),
            dma((2, half)),
            dma((half,)),
            dma((half,)),
            dma((2, half)),
            dma((2, half)),
            dma((2, half)),
            dma((half,)),
            dma((heads,)),
            dma((2,)),
            dma((2,)),
        ],
        compiler_params=pltpu.CompilerParams(
            collective_id=0, has_side_effects=True, vmem_limit_bytes=56 * 2**20),
        name="attend_project",
    )(
        queries.reshape(tokens, features),
        keys.reshape(tokens, features),
        values.reshape(tokens, features),
        out_weight.T.reshape(chunks, width, features),
    )
    return out.reshape(frames_here, rows_here, columns, slots * wide)


def solution(mesh):
    size = dict(mesh.shape)
    pairs = size["rows"] == 2 and size["groups"] == 2 and size["heads"] == 2
    body = general
    if pairs and size["frames"] == 4:
        body = functools.partial(fused, size["frames"])
    return jax.shard_map(
        body,
        mesh=mesh,
        in_specs=(
            P(("groups", "frames"), "rows", None, "heads"),
            P(("groups", "frames"), "rows", None, "heads"),
            P(("groups", "frames"), "rows", None, "heads"),
            P("heads", "frames"),
        ),
        out_specs=P(("groups", "frames"), "rows", None, "heads"),
        check_vma=False,
    )
```

time: 56.6 us -> 50.1 us (0.89)
  the two profiles are of different devices: /device:TPU:24 before, /device:TPU:1 now
where the time goes in v1:
time: 50.1 us; the launch traced here: 49.6 us
  Pallas kernels  47.2 us (94%)
  local copies, waits for them, and re-layouts  2.37 us (5%)
    pallas_call x1, Pallas kernels, fused(): pl.pallas_call(functools.partial(kernel, nz), out_shape=jax.ShapeDtypeStr...  47.2 us
    unnamed x1, local copies, waits for them, and re-layouts  2.37 us

profile of v1, /device:TPU:1, one launch (start us, length us, event | category | flops | bytes accessed | tf_op | source)
XLA Modules:
  0.0 49.6 jit_solution(671135146230600828)
XLA Ops:
  0.0 47.2 %attend_project.1 = bf16[512,1120]{1,0:T(8,128)(2,1)} custom-call(bf16[512,1120]{1,0:T(8,128)(2,1)} %bitcast.9, bf16[512,1120]{1,0:T(8,128)(2,1)} %bitcast.10, bf16[512,1120]{1,0:T(8,128)(2,1)} %bitcast.11, bf16[10,56,1120]{2,1,0:T(8,128)(2,1)} %bitcast.8), custom_call_target="tpu_custom_call" | custom-call | tf_op jit(solution)/shard_map/attend_project/pallas_call | solution.py:476
  47.2 2.4 %copy.6 = bf16[1,8,64,1120]{3,2,1,0:T(8,128)(2,1)} copy(bf16[1,8,64,1120]{3,2,1,0:T(8,128)(2,1)} %bitcast.7) | data formatting | bytes 2293760

commit v2 on v1

--- a/solution.py
+++ b/solution.py
@@ -56,19 +56,19 @@
 
 A, D, X, Y = 0, 1, 2, 3
 PIECES = 5
-OVER_Z, OVER_X, LAG = 1, 2, 3
+OVER_Z, NEAR_X, FAR_X, LAG, LAG_Z = 1, 1, 2, 3, 4
 
 
 def kernel(
     nz, q_hbm, k_hbm, v_hbm, w_ref, out_ref,
     q_ref, k_ref, v_ref, kt, wbuf, att, st, acc, rs_send, rs_recv, hand, z_recv, fin_send, fin, fmat, nmat,
     in_sem, w_recv, own_send, rel_send, block_sem, rs_out, rs_in, hand_out, hand_in, z_out, z_in,
-    ag_out, give_out, fin_in, at_out, at_in,
+    ag_out, fin_in, at_out, at_in,
 ):
     y, z = lax.axis_index("groups"), lax.axis_index("frames")
     x, c = lax.axis_index("rows"), lax.axis_index("heads")
     chunks = w_ref.shape[0]
-    tokens, features = q_ref.shape
+    tokens, features = k_ref.shape
     wide = w_ref.shape[0] * w_ref.shape[1]
     heads = features // HD
     half = heads // 2
@@ -85,6 +85,11 @@
             x if x_ is None else x_,
             c if c_ is None else c_,
         )
+
+    def when(wanted, act):
+        @pl.when(wanted)
+        def _():
+            act()
 
     partner = dev(c_=1 - c)
     barrier = pltpu.get_barrier_semaphore()
@@ -104,10 +109,11 @@
 
     loads = [
         pltpu.make_async_copy(src, dst, in_sem.at[n])
-        for n, (src, dst) in enumerate(((k_hbm, k_ref), (v_hbm, v_ref), (q_hbm, q_ref)))
+        for n, (src, dst) in enumerate(((k_hbm, k_ref), (v_hbm, v_ref), (q_hbm, q_ref.at[c])))
     ]
-    for load in loads:
-        load.start()
+    loads[0].start()
+    loads[1].start()
+    when(c != x, loads[2].start)
 
     pl.semaphore_wait(barrier, jnp.where((z > 0) & (z < nz - 1), 9, 7))
 
@@ -122,11 +128,6 @@
             act(j)
             return carry
         lax.fori_loop(begin, count, body, 0)
-
-    def when(wanted, act):
-        @pl.when(wanted)
-        def _():
-            act()
 
     mine = lax.rem(x + y + c, 2)
     kind = jnp.where(relays, A, D)
@@ -164,10 +165,10 @@
         def _():
             each(OVER_Z, lambda j: act(near_copy(j)))
 
-    near_each(lambda copy: copy.start())
-
     block_local = pltpu.make_async_copy(w_ref, wbuf.at[z, c], block_sem.at[0])
     block_out = remote(w_ref, wbuf.at[z, c], block_sem.at[1], block_sem.at[2], partner)
+    lend = remote(q_hbm, q_ref.at[c], in_sem.at[3], in_sem.at[4], partner)
+    when(relays, lend.start)
     when(home == c, block_local.start)
     when(home != c, block_out.start)
 
@@ -193,9 +194,11 @@
     edge = (z == 0) | (z == nz - 1)
 
     def split(s, j):
-        direct = jnp.where(edge & (jnp.abs(s - z) == 1), OVER_Z, 0)
+        close = jnp.abs(s - z) == 1
+        direct = jnp.where(edge & close, OVER_Z, 0)
+        turned = direct + jnp.where(close, NEAR_X, FAR_X)
         plane = (s > 0) & (s < nz - 1) & (j >= direct)
-        return plane & (j < direct + OVER_X), plane & (j >= direct + OVER_X)
+        return plane & (j < turned), plane & (j >= turned)
 
     def sends_a(s, j):
         ends, more, last, to, at = place(s)
@@ -233,9 +236,9 @@
             else:
                 when(needed, copy.start)
 
-    def on_d(s, j):
+    def on_d(s, j, along):
         options, share = sends_d(s, j)
-        for wanted, what, copy, inner in options:
+        for wanted, what, copy, inner in options[2:] if along else options[:2]:
             @pl.when(wanted)
             def _():
                 arrived(s, what, j)
@@ -288,12 +291,8 @@
                       dev(z_=jnp.minimum(z + 1, nz - 1)))
 
     def across(core, j):
-        return remote(fin_send.at[core, j], fin.at[x * half + j], ag_out.at[core, j], fin_in.at[x * half + j],
-                      dev(x_=1 - x, c_=core))
-
-    def inner(core, j):
-        return remote(fin_send.at[core, j], fin.at[x * half + j], give_out.at[j], fin_in.at[x * half + j],
-                      partner)
+        return remote(fin_send.at[core, j], fin.at[core, x * half + j], ag_out.at[core, j], fin_in.at[core, j],
+                      dev(x_=1 - x, c_=x))
 
     def gather_step(j):
         for core in range(2):
@@ -318,11 +317,7 @@
             fin_send[core, j] = acc[core, j].astype(bf16)
             when(z < nz - 1, up(core, j).start)
             across(core, j).start()
-
-            @pl.when(c == core)
-            def _():
-                fin[x * half + j] = fin_send[core, j]
-            when(c != core, inner(core, j).start)
+            fin[core, x * half + j] = fin_send[core, j]
 
     @pl.when(jnp.logical_not(relays))
     def _():
@@ -338,36 +333,41 @@
         high = min(-(-(-(-end // HD) * HD) // LANES) * LANES, features)
         cuts.append((begin, end, low, high))
 
-    def finished(i):
-        ref = fin.at[i]
-        remote(ref, ref, give_out.at[0], fin_in.at[i], partner).wait_recv()
-
     sections = ((0, 4 * LANES), (4 * LANES, features))
 
     def att_copy(n, rows):
         begin, end = sections[n]
         ref = att.at[rows, :, begin:end]
-        return remote(ref, ref, at_out.at[n], at_in.at[n], partner)
-
-    def attend():
-        each(half, lambda j: finished((1 - x) * half + j))
-        when(relays, lambda: each(half, lambda j: finished(x * half + j)))
+        return remote(ref, ref, at_out.at[rows, n], at_in.at[rows, n], partner)
+
+    def attend(turn):
+        rows = lax.rem(c + turn, 2)
+
+        def finished(j):
+            ref = fin.at[rows, (1 - x) * half + j]
+            remote(ref, ref, ag_out.at[rows, j], fin_in.at[rows, j], partner).wait_recv()
+
+        each(half, finished)
         for h in range(heads):
             own = slice(h * HD, (h + 1) * HD)
-            fmat[own, own] = fin[h, :, :HD]
-            nmat[own, own] = jnp.broadcast_to(fin[h, :, HD:HD + 1], (HD, HD))
+            block = fin[rows, h]
+            fmat[own, own] = block[:, :HD]
+            nmat[own, own] = jnp.broadcast_to(block[:, HD:HD + 1], (HD, HD))
         sent = 0
         for begin, end, low, high in cuts:
-            qp = jnp.maximum(q_ref[:, low:high], 0)
+            qp = jnp.maximum(q_ref[rows, :, low:high], 0)
             numer = jnp.dot(qp, fmat[low:high, begin:end], preferred_element_type=f32)
             denom = jnp.dot(qp, nmat[low:high, begin:end], preferred_element_type=f32)
-            att[c, :, begin:end] = (numer / (denom + EPS)).astype(bf16)
+            att[rows, :, begin:end] = (numer / (denom + EPS)).astype(bf16)
             if end == sections[sent][1]:
-                att_copy(sent, c).start()
+                att_copy(sent, rows).start()
                 sent += 1
 
-    loads[2].wait()
-    turn = jnp.where(relays, parts + (parts - 2) * z, 0)
+    @pl.when(jnp.logical_not(relays))
+    def _():
+        loads[2].wait()
+        remote(q_hbm, q_ref.at[1 - c], in_sem.at[3], in_sem.at[4], partner).wait_recv()
+        each(2, attend)
 
     def step(t):
         d, j = t // parts + 1, lax.rem(t, parts)
@@ -375,17 +375,21 @@
         @pl.when(relays)
         def _():
             when(d < nz, lambda: around(d, lambda s: on_a(s, j)))
-            late = t - LAG
-
-            @pl.when(late >= 0)
-            def _():
-                around(late // parts + 1, lambda s: on_d(s, lax.rem(late, parts)))
-        when(t == turn, attend)
-
-    each((nz - 1) * parts + LAG, step)
-
-    for n in range(len(sections)):
-        att_copy(n, 1 - c).wait_recv()
+            for lag, along in ((LAG, False), (LAG_Z, True)):
+                late = t - lag
+
+                @pl.when((late >= 0) & (late < (nz - 1) * parts))
+                def _():
+                    around(late // parts + 1, lambda s: on_d(s, lax.rem(late, parts), along))
+
+    each((nz - 1) * parts + max(LAG, LAG_Z), step)
+    near_each(lambda copy: copy.start())
+
+    @pl.when(relays)
+    def _():
+        for rows in range(2):
+            for n in range(len(sections)):
+                att_copy(n, rows).wait_recv()
 
     def slot(i):
         s = jnp.where(z <= slots * c, i, slots - 1 - i)
@@ -401,40 +405,63 @@
     def product(rows, weights):
         return lax.dot_general(att[rows], weights, (((1,), (1,)), ((), ())), preferred_element_type=f32)
 
+    def drained(wanted, begin, end):
+        @pl.when(relays & wanted)
+        def _():
+            each(end, lambda t: around(t // parts + 1, lambda s: drain(s, lax.rem(t, parts))), begin)
+
     width = wide // 2
-    for i in range(slots):
+
+    def quarter(source, rows, first):
+        return wbuf[source, rows, pl.ds(first, parts)].reshape(width, features)
+
+    def await_all(source, kinds):
+        each(parts, lambda j: landed(source, j, kinds))
+
+    def put(s, side, value):
+        value = value.astype(out_ref.dtype)
+        for at in range(slots):
+            for part in range(2):
+                first = (at * 2 + part) * width
+
+                @pl.when((s == at) & (side == part))
+                def _():
+                    out_ref[:, first:first + width] = value
+
+    def near(i):
         s, source = slot(i)
-
-        def quarter(rows, first):
-            return wbuf[source, rows, pl.ds(first, parts)].reshape(width, features)
-
-        def await_all(kinds):
-            @pl.when(source != z)
-            def _():
-                each(parts, lambda j: landed(source, j, kinds))
-
-        @pl.when(source == z)
-        def _():
-            block_local.wait()
-            other = wbuf.at[z, 1 - c]
-            remote(w_ref, other, block_sem.at[1], block_sem.at[2], partner).wait_recv()
-
-        def put(side, value):
-            value = value.astype(out_ref.dtype)
-            for at in range(slots):
-                for part in range(2):
-                    first = (at * 2 + part) * width
-
-                    @pl.when((s == at) & (side == part))
-                    def _():
-                        out_ref[:, first:first + width] = value
-
-        await_all((A, X))
-        put(y, product(x, quarter(x, y * parts)) + product(1 - x, quarter(1 - x, y * parts)))
-        await_all((Y,))
-        rest = product(x, quarter(x, (1 - y) * parts))
-        await_all((D,))
-        put(1 - y, rest + product(1 - x, quarter(1 - x, (1 - y) * parts)))
+        await_all(source, (A, X))
+        put(s, y, product(x, quarter(source, x, y * parts)) + product(1 - x, quarter(source, 1 - x, y * parts)))
+
+    def distant(i):
+        s, source = slot(i)
+        await_all(source, (D,))
+        rest = product(1 - x, quarter(source, 1 - x, (1 - y) * parts))
+        await_all(source, (Y,))
+        put(s, 1 - y, rest + product(x, quarter(source, x, (1 - y) * parts)))
+
+    @pl.when(home == c)
+    def _():
+        s, source = slot(0)
+        block_local.wait()
+        other = wbuf.at[z, 1 - c]
+        remote(w_ref, other, block_sem.at[1], block_sem.at[2], partner).wait_recv()
+        out = product(0, wbuf[source, 0].reshape(wide, features))
+        out = (out + product(1, wbuf[source, 1].reshape(wide, features))).astype(out_ref.dtype)
+        for at in range(slots):
+            @pl.when(s == at)
+            def _():
+                out_ref[:, at * wide:(at + 1) * wide] = out
+
+    @pl.when(home != c)
+    def _():
+        near(0)
+
+    drained(edge, 0, (nz - 2) * parts)
+    when(home != c, lambda: distant(0))
+    near(slots - 1)
+    drained(edge, (nz - 2) * parts, (nz - 1) * parts)
+    distant(slots - 1)
 
     near_each(lambda copy: copy.wait_send())
     when(relays | (z == 0) | (z == nz - 1), lambda: own_each(lambda copy: copy.wait_send()))
@@ -449,17 +476,16 @@
             for core in range(2):
                 when(z < nz - 1, up(core, j).wait_send)
                 across(core, j).wait_send()
-                when(c != core, inner(core, j).wait_send)
-
+
+    drained(jnp.logical_not(edge), 0, (nz - 1) * parts)
     each(half, sent)
-    for n in range(len(sections)):
-        att_copy(n, c).wait_send()
-
-    @pl.when(relays)
+    when(relays, lend.wait_send)
+
+    @pl.when(jnp.logical_not(relays))
     def _():
-        def drained(t):
-            around(t // parts + 1, lambda s: drain(s, lax.rem(t, parts)))
-        each((nz - 1) * parts, drained)
+        for rows in range(2):
+            for n in range(len(sections)):
+                att_copy(n, rows).wait_send()
 
 
 def fused(nz, queries, keys, values, out_weight):
@@ -473,13 +499,16 @@
     vmem, hbm = pl.BlockSpec(memory_space=pltpu.VMEM), pl.BlockSpec(memory_space=pl.ANY)
     bf16, f32 = jnp.bfloat16, jnp.float32
     dma = pltpu.SemaphoreType.DMA
+    def keep(array):
+        return pltpu.with_memory_space_constraint(array, pltpu.HBM)
+
     out = pl.pallas_call(
         functools.partial(kernel, nz),
         out_shape=jax.ShapeDtypeStruct((tokens, slots * wide), bf16),
         in_specs=[hbm] * 4,
         out_specs=vmem,
         scratch_shapes=[
-            pltpu.VMEM((tokens, features), bf16),
+            pltpu.VMEM((2, tokens, features), bf16),
             pltpu.VMEM((tokens, features), bf16),
             pltpu.VMEM((tokens, features), bf16),
             pltpu.VMEM((features, tokens), bf16),
@@ -492,10 +521,10 @@
             pltpu.VMEM((half, HD, LANES), bf16),
             pltpu.VMEM((2, half, HD, LANES), bf16),
             pltpu.VMEM((2, half, HD, LANES), bf16),
-            pltpu.VMEM((heads, HD, LANES), bf16),
+            pltpu.VMEM((2, heads, HD, LANES), bf16),
             pltpu.VMEM((features, features), bf16),
             pltpu.VMEM((features, features), bf16),
-            dma((3,)),
+            dma((5,)),
             dma((nz, 4, parts)),
             dma((3, parts)),
             dma((nz, 6, parts)),
@@ -507,19 +536,18 @@
             dma((2, half)),
             dma((2, half)),
             dma((2, half)),
-            dma((half,)),
-            dma((heads,)),
-            dma((2,)),
-            dma((2,)),
+            dma((2, half)),
+            dma((2, 2)),
+            dma((2, 2)),
         ],
         compiler_params=pltpu.CompilerParams(
-            collective_id=0, has_side_effects=True, vmem_limit_bytes=56 * 2**20),
+            collective_id=0, has_side_effects=True, vmem_limit_bytes=30 * 2**20),
         name="attend_project",
     )(
-        queries.reshape(tokens, features),
-        keys.reshape(tokens, features),
-        values.reshape(tokens, features),
-        out_weight.T.reshape(chunks, width, features),
+        keep(queries.reshape(tokens, features)),
+        keep(keys.reshape(tokens, features)),
+        keep(values.reshape(tokens, features)),
+        keep(out_weight.T.reshape(chunks, width, features)),
     )
     return out.reshape(frames_here, rows_here, columns, slots * wide)
 

time: 50.1 us -> 46.5 us (0.928)
  Pallas kernels: 47.2 us -> 45.4 us
  local copies, waits for them, and re-layouts: 2.37 us -> 1.02 us
    pallas_call x1, Pallas kernels: 47.2 us -> 45.4 us  [fused(): pl.pallas_call(functools.partial(kernel, nz), out_shape=jax.ShapeDtypeStr...]
    unnamed x1, local copies, waits for them, and re-layouts: 2.37 us -> 1.02 us
where the time goes in v2:
time: 46.5 us; the launch traced here: 46.4 us
  Pallas kernels  45.4 us (98%)
  local copies, waits for them, and re-layouts  1.02 us (2%)
    pallas_call x1, Pallas kernels, fused(): pl.pallas_call(functools.partial(kernel, nz), out_shape=jax.ShapeDtypeStr...  45.4 us
    unnamed x1, local copies, waits for them, and re-layouts  1.02 us

profile of v2, /device:TPU:1, one launch (start us, length us, event | category | flops | bytes accessed | tf_op | source)
XLA Modules:
  0.0 46.4 jit_solution(15147103883057204171)
XLA Ops:
  0.0 45.4 %attend_project.1 = bf16[512,1120]{1,0:T(8,128)(2,1)S(1)} custom-call(bf16[512,1120]{1,0:T(8,128)(2,1)} %bitcast.9, bf16[512,1120]{1,0:T(8,128)(2,1)} %bitcast.10, bf16[512,1120]{1,0:T(8,128)(2,1)} %bitcast.11, bf16[10,56,1120]{2,1,0:T(8,128)(2,1)} %bitcast.8), custom_call_target="tpu_custom_call" | custom-call | tf_op jit(solution)/shard_map/attend_project/pallas_call | solution.py:505
  45.4 1.0 %copy.6 = bf16[1,8,64,1120]{3,2,1,0:T(8,128)(2,1)} copy(bf16[1,8,64,1120]{3,2,1,0:T(8,128)(2,1)S(1)} %bitcast.7) | data formatting | bytes 2293760

commit v3 on v2

--- a/solution.py
+++ b/solution.py
@@ -56,7 +56,8 @@
 
 A, D, X, Y = 0, 1, 2, 3
 PIECES = 5
-OVER_Z, NEAR_X, FAR_X, LAG, LAG_Z = 1, 1, 2, 3, 4
+OVER_Z, NEAR_X, FAR_X = 3, 1, 2
+LAG, LAG_MID, LAG_Z = 3, 10, 5
 
 
 def kernel(
@@ -375,7 +376,7 @@
         @pl.when(relays)
         def _():
             when(d < nz, lambda: around(d, lambda s: on_a(s, j)))
-            for lag, along in ((LAG, False), (LAG_Z, True)):
+            for lag, along in ((jnp.where(edge, LAG, LAG_MID), False), (LAG_Z, True)):
                 late = t - lag
 
                 @pl.when((late >= 0) & (late < (nz - 1) * parts))

time: 46.5 us -> 45.7 us (0.983); the launches traced: 46.4 us -> 44.9 us
  Pallas kernels: 45.4 us -> 43.8 us
    pallas_call x1, Pallas kernels: 45.4 us -> 43.8 us  [fused(): pl.pallas_call(functools.partial(kernel, nz), out_shape=jax.ShapeDtypeStr...]
where the time goes in v3:
time: 45.7 us; the launch traced here: 44.9 us
  Pallas kernels  43.8 us (96%)
  local copies, waits for them, and re-layouts  1.02 us (2%)
    pallas_call x1, Pallas kernels, fused(): pl.pallas_call(functools.partial(kernel, nz), out_shape=jax.ShapeDtypeStr...  43.8 us
    unnamed x1, local copies, waits for them, and re-layouts  1.02 us

profile of v3, /device:TPU:1, one launch (start us, length us, event | category | flops | bytes accessed | tf_op | source)
XLA Modules:
  0.0 44.9 jit_solution(4786954498236499955)
XLA Ops:
  0.0 43.8 %attend_project.1 = bf16[512,1120]{1,0:T(8,128)(2,1)S(1)} custom-call(bf16[512,1120]{1,0:T(8,128)(2,1)} %bitcast.9, bf16[512,1120]{1,0:T(8,128)(2,1)} %bitcast.10, bf16[512,1120]{1,0:T(8,128)(2,1)} %bitcast.11, bf16[10,56,1120]{2,1,0:T(8,128)(2,1)} %bitcast.8), custom_call_target="tpu_custom_call" | custom-call | tf_op jit(solution)/shard_map/attend_project/pallas_call | solution.py:506
  43.9 1.0 %copy.6 = bf16[1,8,64,1120]{3,2,1,0:T(8,128)(2,1)} copy(bf16[1,8,64,1120]{3,2,1,0:T(8,128)(2,1)S(1)} %bitcast.7) | data formatting | bytes 2293760

commit v4 on v3

--- a/solution.py
+++ b/solution.py
@@ -284,8 +284,10 @@
         rs(j).start()
         when(relays, give(j).start)
 
-    fmat[...] = jnp.zeros_like(fmat)
-    nmat[...] = jnp.zeros_like(nmat)
+    @pl.when(jnp.logical_not(relays))
+    def _():
+        fmat[...] = jnp.zeros_like(fmat)
+        nmat[...] = jnp.zeros_like(nmat)
 
     def up(core, j):
         return remote(fin_send.at[core, j], z_recv.at[core, j], z_out.at[core, j], z_in.at[core, j],
@@ -461,8 +463,9 @@
     drained(edge, 0, (nz - 2) * parts)
     when(home != c, lambda: distant(0))
     near(slots - 1)
-    drained(edge, (nz - 2) * parts, (nz - 1) * parts)
+    drained(edge & (home != c), (nz - 2) * parts, (nz - 1) * parts)
     distant(slots - 1)
+    drained(edge & (home == c), (nz - 2) * parts, (nz - 1) * parts)
 
     near_each(lambda copy: copy.wait_send())
     when(relays | (z == 0) | (z == nz - 1), lambda: own_each(lambda copy: copy.wait_send()))

time: 45.7 us -> 45.7 us (level)
  no operation moved by 1% of the time
where the time goes in v4:
time: 45.7 us; the launch traced here: 44.9 us
  Pallas kernels  43.9 us (96%)
  local copies, waits for them, and re-layouts  1.02 us (2%)
    pallas_call x1, Pallas kernels, fused(): pl.pallas_call(functools.partial(kernel, nz), out_shape=jax.ShapeDtypeStr...  43.9 us
    unnamed x1, local copies, waits for them, and re-layouts  1.02 us

profile of v4, /device:TPU:1, one launch (start us, length us, event | category | flops | bytes accessed | tf_op | source)
XLA Modules:
  0.0 44.9 jit_solution(731503281516726024)
XLA Ops:
  0.0 43.9 %attend_project.1 = bf16[512,1120]{1,0:T(8,128)(2,1)S(1)} custom-call(bf16[512,1120]{1,0:T(8,128)(2,1)} %bitcast.9, bf16[512,1120]{1,0:T(8,128)(2,1)} %bitcast.10, bf16[512,1120]{1,0:T(8,128)(2,1)} %bitcast.11, bf16[10,56,1120]{2,1,0:T(8,128)(2,1)} %bitcast.8), custom_call_target="tpu_custom_call" | custom-call | tf_op jit(solution)/shard_map/attend_project/pallas_call | solution.py:509
  43.9 1.0 %copy.6 = bf16[1,8,64,1120]{3,2,1,0:T(8,128)(2,1)} copy(bf16[1,8,64,1120]{3,2,1,0:T(8,128)(2,1)S(1)} %bitcast.7) | data formatting | bytes 2293760
